TPU v7x, 32 devices: a whole 2x2x4 slice. The times are simulated.
32 devices in a mesh: groups: 2 (over x), ctx: 16 (over z, y, core).
Axes of the slice: x: 2, y: 2, z: 4, core: 2. Of those that a mesh axis runs over, the one named last changes fastest.
Arguments:
- conv_input: bfloat16 [4096, 5120], P(('groups', 'ctx')), parts along dimension 0, may hold values from -6 to 6
- step_raw: float32 [4096, 64], P(('groups', 'ctx')), parts along dimension 0, may hold values from -5 to 5.5
- step_bias: float32 [64], replicated, may hold values from -14 to -2
- decay_log: float32 [64], replicated, may hold values from -3 to 0.7
- skip_gain: float32 [64], replicated, may hold values from 0.5 to 1.5
- conv_weight: float32 [4, 5120], replicated, may hold values from -3 to 3
- conv_bias: float32 [5120], replicated, may hold values from -1 to 0.5
- doc_lengths: int32 [8], P('groups'), parts along dimension 0, may hold values from 1 to 1024, 2048 in all
- grad_out: bfloat16 [4096, 4096], P(('groups', 'ctx')), parts along dimension 0, may hold values from -400 to 400
Outputs:
- mixer_out: bfloat16 [4096, 4096], P(('groups', 'ctx')), parts along dimension 0
- grad_input: bfloat16 [4096, 5120], P(('groups', 'ctx')), parts along dimension 0
- grad_step: float32 [4096, 64], P(('groups', 'ctx')), parts along dimension 0
- grad_conv: float32 [10, 5120], P('groups'), parts along dimension 0
- grad_heads: float32 [6, 64], P('groups'), parts along dimension 0
There are 2 independent parts, one for each index of `groups`. A program takes and returns all parts, laid end to end along the dimension named above; an argument that names none is the same for every part. Nothing has to cross between parts.
Inputs may be any that keep to these rules, and one draw needn't show every extreme that they name: doc_lengths lists the lengths of the 4 documents that follow one another from token 0; they sum to 2048, and the longest has exactly 1024 tokens.
All inputs are finite; a program needn't handle non-finite values.
Results may differ from a plain program's by a relative error of at most 0.001.
Values may be sent and summed in bfloat16 or wider, within the bound.
No kernel may reach another device: no remote copies, remote signals or barrier semaphores. Data moves between devices by JAX's collectives and lax.ppermute only.
A program may use at most 192 MiB of HBM per device.

v0:
```python
from functools import partial
import math
import jax
import jax.numpy as jnp
from jax import lax
from jax.sharding import PartitionSpec as P

GROUPS = 4
HIGH = lax.Precision.HIGHEST


def passed_along(value, axis, steps):
    count = lax.axis_size(axis)
    initial, last = (max(0, -steps), min(count, count - steps))
    return lax.ppermute(value, axis, [(source, source + steps) for source in range(initial, last)])


def doc_offsets(doc_lengths, positions):
    ends = jnp.cumsum(doc_lengths, dtype=jnp.int32)
    starts = ends - doc_lengths
    before = starts[None, :] <= positions[:, None]
    opening = jnp.max(jnp.where(before, starts[None, :], 0), axis=1)
    return positions - opening


def convolve(extended, conv_weight, conv_bias, inside):
    count = inside.shape[0]
    taps = conv_weight.shape[0]
    total = jnp.zeros((count, extended.shape[1]), jnp.float32) + conv_bias[None, :]
    for lag in range(taps):
        reach = taps - 1 - lag
        valid = (inside >= reach).astype(jnp.float32)[:, None]
        total = total + conv_weight[lag][None, :] * extended[lag : lag + count] * valid
    return jax.nn.silu(total)


def prepare(
    extended, step_raw, step_bias, decay_log, skip_gain, conv_weight, conv_bias, inside, layout
):
    groups, headdim, block = layout
    length, heads = step_raw.shape
    share = heads // groups
    count = length // block
    inner = heads * headdim
    act = convolve(extended, conv_weight, conv_bias, inside)
    width = (act.shape[1] - inner) // 2
    inputs = act[:, :inner].reshape(count, block, groups, share, headdim)
    b_values = act[:, inner : inner + width].reshape(count, block, groups, width // groups)
    c_values = act[:, inner + width :].reshape(count, block, groups, width // groups)
    step_size = jax.nn.softplus(step_raw + step_bias[None, :])
    log_rate = (-step_size * jnp.exp(decay_log)[None, :]).reshape(count, block, groups, share)
    cum_decay = jnp.cumsum(log_rate, axis=1)
    return (
        inputs,
        b_values,
        c_values,
        step_size.reshape(count, block, groups, share),
        cum_decay,
        skip_gain.reshape(groups, share),
    )


def state_part(inputs, b_values, step_size, cum_decay, doc_count):
    whole = jnp.exp(cum_decay[:, -1]) * (doc_count[:, -1] == 0)[:, None, None]
    tail = (
        jnp.exp(cum_decay[:, -1:] - cum_decay) * (doc_count == doc_count[:, -1:])[:, :, None, None]
    )
    local = jnp.einsum(
        "cqgrp,cqgn->cgrpn", inputs * (tail * step_size)[..., None], b_values, precision=HIGH
    )

    def carry_step(carried, pieces):
        scale, state = carried
        factor, piece = pieces
        return ((factor * scale, factor[..., None, None] * state + piece), (scale, state))

    initial = (jnp.ones(whole.shape[1:], jnp.float32), jnp.zeros(local.shape[1:], jnp.float32))
    final, chains = lax.scan(carry_step, initial, (whole, local))
    return (final[0], final[1], chains[0], chains[1])


def out_part(
    inputs, b_values, c_values, step_size, cum_decay, skip_heads, a_chain, b_chain, doc_count
):
    block = doc_count.shape[1]
    order = jnp.arange(block, dtype=jnp.int32)
    allowed = (doc_count[:, :, None] == doc_count[:, None, :]) & (order[:, None] >= order[None, :])[
        None
    ]
    by_head = jnp.moveaxis(cum_decay, 1, -1)
    spread = by_head[..., :, None] - by_head[..., None, :]
    decay = jnp.exp(jnp.where(allowed[:, None, None], spread, -1e30))
    scores = jnp.einsum("ctgn,csgn->cgts", c_values, b_values, precision=HIGH)
    weights = scores[:, :, None] * decay * jnp.moveaxis(step_size, 1, -1)[..., None, :]
    y_diag = jnp.einsum("cgrts,csgrp->ctgrp", weights, inputs, precision=HIGH)
    head_in = jnp.exp(cum_decay) * (doc_count == 0)[:, :, None, None]
    y_carry = head_in[..., None] * jnp.einsum(
        "ctgn,cgrpn->ctgrp", c_values, b_chain, precision=HIGH
    )
    mixed = y_diag + y_carry + skip_heads[None, None, :, :, None] * inputs
    return (mixed, head_in * a_chain[:, None])


def outer_part(c_values, head_reach, state_in):
    return head_reach[..., None] * jnp.einsum(
        "ctgn,grpn->ctgrp", c_values, state_in, precision=HIGH
    )


def owner_join(earlier, later):
    factor_early, value_early = earlier
    factor_late, value_late = later
    return (factor_late * factor_early, factor_late * value_early + value_late)


def owner_prefix(pieces, reverse):
    values, factors = pieces
    scales, totals = lax.associative_scan(owner_join, (factors, values), reverse=reverse, axis=1)
    blank = jnp.zeros_like(totals[:, :1])
    if reverse:
        return jnp.concatenate([totals[:, 1:], blank], axis=1)
    return jnp.concatenate([blank, totals[:, :-1]], axis=1)


def body(
    conv_input,
    step_raw,
    step_bias,
    decay_log,
    skip_gain,
    conv_weight,
    conv_bias,
    doc_lengths,
    grad_out,
):
    length, feature_lanes = conv_input.shape
    heads = step_raw.shape[1]
    taps = conv_weight.shape[0]
    inner = grad_out.shape[1]
    headdim = inner // heads
    groups = GROUPS
    devices = lax.axis_size("ctx")
    block = math.gcd(length, 64)
    count = length // block
    border = length - taps + 1
    rim_rows = passed_along(conv_input[border:], "ctx", 1)
    extended = jnp.concatenate([rim_rows, conv_input], axis=0).astype(jnp.float32)
    positions = lax.axis_index("ctx") * length + jnp.arange(length, dtype=jnp.int32)
    inside = doc_offsets(doc_lengths, positions)
    doc_count = jnp.cumsum((inside == 0).astype(jnp.float32).reshape(count, block), axis=1)
    layout = (groups, headdim, block)
    prepared, prep_pull = jax.vjp(
        partial(prepare, inside=inside, layout=layout),
        extended,
        step_raw,
        step_bias,
        decay_log,
        skip_gain,
        conv_weight,
        conv_bias,
    )
    inputs, b_values, c_values, step_size, cum_decay, skip_heads = prepared
    summary, state_pull = jax.vjp(
        partial(state_part, doc_count=doc_count), inputs, b_values, step_size, cum_decay
    )
    decay_all, state_all, a_chain, b_chain = summary
    local_out, out_pull = jax.vjp(
        partial(out_part, doc_count=doc_count),
        inputs,
        b_values,
        c_values,
        step_size,
        cum_decay,
        skip_heads,
        a_chain,
        b_chain,
    )
    y_local, head_reach = local_out
    rates = jnp.broadcast_to(decay_all.reshape(heads, 1, 1), (heads, devices, 1))
    flat_states = state_all.reshape(heads, devices, -1)
    ready = owner_prefix(
        (
            lax.all_to_all(flat_states, "ctx", split_axis=1, concat_axis=1, tiled=True),
            lax.all_to_all(rates, "ctx", split_axis=1, concat_axis=1, tiled=True),
        ),
        False,
    )
    state_in = lax.all_to_all(ready, "ctx", split_axis=1, concat_axis=1, tiled=True).reshape(
        state_all.shape
    )
    y_state, exterior_vjp_fn = jax.vjp(outer_part, c_values, head_reach, state_in)
    mixer_out = (y_local + y_state).reshape(length, inner).astype(jnp.bfloat16)
    upstream = grad_out.astype(jnp.float32).reshape(y_local.shape)
    grad_c_outer, grad_reach, incoming_state_gradient = exterior_vjp_fn(upstream)
    pulled_out = out_pull((upstream, grad_reach))
    grad_inputs, grad_b, grad_c, grad_steps, grad_cum, grad_skip, grad_a_chain, grad_b_chain = (
        pulled_out
    )
    flat_grads = incoming_state_gradient.reshape(heads, devices, -1)
    ready = owner_prefix(
        (
            lax.all_to_all(flat_grads, "ctx", split_axis=1, concat_axis=1, tiled=True),
            lax.all_to_all(rates, "ctx", split_axis=1, concat_axis=1, tiled=True),
        ),
        True,
    )
    adjoint = lax.all_to_all(ready, "ctx", split_axis=1, concat_axis=1, tiled=True).reshape(
        state_all.shape
    )
    grad_decay_all = jnp.sum(adjoint * state_in, axis=(2, 3))
    grad_inputs_two, grad_b_two, grad_steps_two, grad_cum_two = state_pull(
        (grad_decay_all, adjoint, grad_a_chain, grad_b_chain)
    )
    pulled = prep_pull(
        (
            grad_inputs + grad_inputs_two,
            grad_b + grad_b_two,
            grad_c + grad_c_outer,
            grad_steps + grad_steps_two,
            grad_cum + grad_cum_two,
            grad_skip,
        )
    )
    grad_extended, grad_step, grad_bias, grad_log, grad_gain, grad_kernel, grad_kernel_bias = pulled
    returned = passed_along(grad_extended[: taps - 1], "ctx", -1)
    own_rows = grad_extended[taps - 1 :]
    grad_input = jnp.concatenate([own_rows[:border], own_rows[border:] + returned], axis=0).astype(
        jnp.bfloat16
    )
    totals = lax.psum(
        (
            jnp.concatenate([grad_kernel, grad_kernel_bias[None, :]], axis=0),
            jnp.stack([grad_bias, grad_log, grad_gain]),
        ),
        "ctx",
    )
    scale = (length * devices) ** (-0.5)
    return (mixer_out, grad_input, grad_step, totals[0] * scale, totals[1] * scale)


def solution(mesh):
    placed = (
        P(("groups", "ctx"), None),
        P(("groups", "ctx"), None),
        P(),
        P(),
        P(),
        P(),
        P(),
        P("groups"),
        P(("groups", "ctx"), None),
    )
    return jax.shard_map(
        body,
        mesh=mesh,
        in_specs=placed,
        out_specs=(
            P(("groups", "ctx"), None),
            P(("groups", "ctx"), None),
            P(("groups", "ctx"), None),
            P("groups", None),
            P("groups", None),
        ),
        check_vma=False,
    )
```

profile of v0, /device:TPU:8, one launch (start us, length us, event | category | flops | bytes accessed | tf_op | source)
XLA Modules:
  0.0 590.7 jit_solution(1007790423436295223)
XLA Ops:
  19.5 3.2 fusion.41
  25.8 4.7 reshape.284
  30.4 5.8 copy.292
  37.3 7.0 %fusion.35 = f32[2,4,16,64,128]{4,3,2,1,0:T(8,128)} fusion(f32[2,64,4,16,64]{1,4,3,2,0:T(8,128)} %copy.292, f32[2,64,4,16]{1,3,2,0:T(8,128)S(1)} %copy_multiply_fusion, f32[2,64,4,128,1]{3,2,1,0,4:T(4,128)S(1)} %bitcast.262), kind=kOutput, calls=%fused_computation.60 | convolution fusion | flops 805830656 | bytes 6586368 | tf_op jit(solution)/shard_map/jvp(cqgrp,cqgn->cgrpn)/dot_general | solution.py:68
  46.8 6.6 %while.40 = (s32[]{:T(128)}, f32[4,16]{1,0:T(4,128)S(1)}, f32[4,16,64,128]{3,2,1,0:T(8,128)S(1)}, f32[2,4,16]{2,1,0:T(4,128)S(1)}, f32[2,4,16,64,128]{4,3,2,1,0:...) while((s32[]{:T(128)}, f32[4,16]{1,0:T(4,128)S(1)}, ...), condition=%wide.region_5.6_spmd.clone, body=%wide.region_4.5_spmd.clone.sunk | while | flops 2097347 | bytes 27272616 | solution.py:78
  54.1 6.6 %all-to-all-start.1 = ((f32[64,16,1]{0,2,1:T(1,128)}), f32[64,16,1]{0,2,1:T(1,128)S(1)}, u32[]{:S(2)}, u32[]{:S(2)}) async-start(f32[64,16,1]{0,2,1:T(1,128)} %broadcast_in_dim.115), calls=%async_computation.1 | async-start | bytes 16384 | tf_op jit(solution)/shard_map/all_to_all | solution.py:184
  62.3 4.2 copy.300
  66.4 6.6 %all-to-all-start = ((f32[64,16,512]{2,0,1:T(8,128)}), f32[64,16,512]{2,0,1:T(8,128)S(1)}, u32[]{:S(2)}, u32[]{:S(2)}) async-start(f32[64,16,512]{2,0,1:T(8,128)} %copy.300), calls=%async_computation | async-start | bytes 4194304 | tf_op jit(solution)/shard_map/all_to_all | solution.py:183
  75.4 43.4 %all-to-all-done = f32[64,16,512]{2,0,1:T(8,128)S(1)} async-done(((f32[64,16,512]{2,0,1:T(8,128)}), f32[64,16,512]{2,0,1:T(8,128)S(1)}, u32[]{:S(2)}, u32[]{:S(2)}) %all-to-all-start) | async-done | bytes 2097184 | tf_op jit(solution)/shard_map/all_to_all | solution.py:183
  130.8 4.1 pad.96
  136.7 4.1 pad.95
  144.1 4.1 pad.143
  148.1 3.9 pad.221
  155.5 6.4 %all-to-all-start.2 = ((f32[64,16,512]{2,0,1:T(8,128)}), f32[64,16,512]{2,0,1:T(8,128)S(1)}, u32[]{:S(2)}, u32[]{:S(2)}) async-start(f32[64,16,512]{2,0,1:T(8,128)} %concatenate.38), calls=%async_computation.2 | async-start | bytes 4194304 | tf_op jit(solution)/shard_map/all_to_all | solution.py:188
  161.9 3.3 reshape.291
  165.3 5.9 %copy.305 = f32[2,64,4,16,64]{1,4,3,2,0:T(8,128)} copy(f32[2,64,4,16,64]{4,3,2,1,0:T(8,128)} %reshape.291) | data formatting | bytes 4194304 | tf_op jit(solution)/shard_map/reshape | solution.py:193
  171.3 36.5 %all-to-all-done.2 = f32[64,16,512]{2,0,1:T(8,128)S(1)} async-done(((f32[64,16,512]{2,0,1:T(8,128)}), f32[64,16,512]{2,0,1:T(8,128)S(1)}, u32[]{:S(2)}, u32[]{:S(2)}) %all-to-all-start.2) | async-done | bytes 2097184 | tf_op jit(solution)/shard_map/all_to_all | solution.py:188
  213.3 3.7 fusion.90
  217.0 10.0 %fusion.22 = (f32[2,64,4,16]{1,3,2,0:T(8,128)}, f32[2,64,4,16]{1,3,2,0:T(8,128)S(1)}, f32[2,4,16,64,64]{4,3,2,1,0:T(8,128)}) fusion(f32[2,64,4,16,64]{1,4,3,2,0:T(8,128)S(1)} %copy-done, f32[4,16,64,2,64]{4,2,1,0,3:T(8,128)S(1)} %fusion.90, f32[2,4,16,64,128]{4,3,2,1,0:T(8,128)} %get-tuple-element.578, f32[2,64,4,128,1]{3,2,1,0,4:T(4,128)S(1)} %bitcast.257), kind=kOutput, calls=%fused_computation.45 | convolution fusion | flops 807387136 | bytes 10813440 | tf_op jit(solution)/shard_map/jvp(ctgn,cgrpn->ctgrp)/dot_general | solution.py:97
  227.7 3.6 fusion.23
  235.7 4.1 copy.317
  239.8 6.6 %all-to-all-start.3 = ((f32[64,16,512]{2,0,1:T(8,128)}), f32[64,16,512]{2,0,1:T(8,128)}, u32[]{:S(2)}, u32[]{:S(2)}) async-start(f32[64,16,512]{2,0,1:T(8,128)} %copy.317), calls=%async_computation.3 | async-start | bytes 4194304 | tf_op jit(solution)/shard_map/all_to_all | solution.py:202
  246.5 45.7 %all-to-all-done.3 = f32[64,16,512]{2,0,1:T(8,128)} async-done(((f32[64,16,512]{2,0,1:T(8,128)}), f32[64,16,512]{2,0,1:T(8,128)}, u32[]{:S(2)}, u32[]{:S(2)}) %all-to-all-start.3) | async-done | bytes 2097184 | tf_op jit(solution)/shard_map/all_to_all | solution.py:202
  304.4 4.1 pad.105
  318.2 6.4 %pad.145 = f32[64,15,512]{2,0,1:T(8,128)} pad(f32[64,8,512]{2,0,1:T(8,128)} %pad_maximum_fusion.2, f32[]{:T(128)} %constant.116.clone.1), padding=0_0_0x0_0_1x0_0_0 | pad | bytes 3014660 | tf_op jit(solution)/shard_map/slice | solution.py:121
  324.6 6.5 %pad.222 = f32[64,16,512]{2,0,1:T(8,128)} pad(f32[64,8,512]{2,0,1:T(8,128)} %add.278, f32[]{:T(128)} %constant.116.clone.1), padding=0_0_0x1_0_1x0_0_0 | pad | bytes 3145732
  331.1 3.9 slice_add_fusion.7
  341.2 6.6 %all-to-all-start.4 = ((f32[64,16,512]{2,0,1:T(8,128)}), f32[64,16,512]{2,0,1:T(8,128)}, u32[]{:S(2)}, u32[]{:S(2)}) async-start(f32[64,16,512]{2,0,1:T(8,128)} %concatenate.42), calls=%async_computation.4 | async-start | bytes 4194304 | tf_op jit(solution)/shard_map/all_to_all | solution.py:207
  347.8 4.5 reshape.292
  352.5 4.9 copy.307
  358.8 9.6 %fusion.43 = (f32[2,4,16,64]{3,2,1,0:T(8,128)}, f32[2,4,16,64]{3,2,1,0:T(8,128)}, f32[2,4,16,64]{3,2,1,0:T(8,128)}, f32[2,4,64,64]{3,2,1,0:T(8,128)}) fusion(f32[2,4,16,64]{3,2,1,0:T(8,128)S(1)} %copy.291, f32[2,4,16,64]{3,2,1,0:T(8,128)S(1)} %copy.289, f32[2,4,64,64]{3,2,1,0:T(8,128)S(1)} %fusion.85, pred[2,64,64]{2,1,0:T(8,128)(4,1)S(1)} %compare_and_fusion, ...), kind=kOutput, calls=%fused_computation.79 | convolution fusion | flops 409411584 | bytes 3579904 | tf_op jit(solution)/shard_map/transpose(jvp(cgrts,csgrp->ctgrp))/dot_general | solution.py:95
  368.5 9.6 %fusion.18 = bf16[2,64,4,16,64]{1,4,3,2,0:T(8,128)(2,1)} fusion(f32[4,16,64,2,64]{4,2,1,0,3:T(8,128)S(1)} %copy-done.14, f32[2,4,16,64,64]{4,3,2,1,0:T(8,128)S(1)} %copy-done.17, f32[2,64,4,16,64]{1,4,3,2,0:T(8,128)S(1)} %copy-done.6, f32[2,64,4,16]{1,3,2,0:T(8,128)S(1)} %copy-done.39, f32[4,16]{1,0:T(4,128)S(1)} %mul.662, ...), kind=kOutput, calls=%fused_computation.39 | convolution fusion | flops 408420352 | bytes 7610624 | tf_op jit(solution)/shard_map/jvp(cgrts,csgrp->ctgrp)/dot_general | solution.py:95
  378.1 5.3 copy.304
  383.4 4.5 convert_element_type.79
  387.9 9.1 %convolution_bitcast_fusion.1 = f32[2,64,4,128]{3,1,2,0:T(8,128)S(1)} fusion(f32[4,16,64,128,1]{3,2,1,0,4:T(8,128)S(1)} %reshape.310, f32[2,64,4,16,64]{1,4,3,2,0:T(8,128)} %copy.305, f32[2,64,4,16]{1,3,2,0:T(8,128)S(1)} %copy-done.39), kind=kOutput, calls=%fused_computation.108 | convolution fusion | flops 805830656 | bytes 4489216 | tf_op jit(solution)/shard_map/transpose(jvp(ctgn,grpn->ctgrp))/dot_general | solution.py:105
  397.1 8.9 %fusion.70 = f32[2,4,64,128]{3,2,1,0:T(8,128)S(1)} fusion(f32[2,4,16,64,128]{4,3,2,1,0:T(8,128)} %get-tuple-element.578, f32[2,64,4,16,64]{1,4,3,2,0:T(8,128)S(1)} %copy-done.1, f32[2,64,4,16]{1,3,2,0:T(8,128)S(1)} %get-tuple-element.358), kind=kOutput, calls=%fused_computation.105 | convolution fusion | flops 805830656 | bytes 6586368 | tf_op jit(solution)/shard_map/transpose(jvp(ctgn,cgrpn->ctgrp))/dot_general | solution.py:97
  407.3 5.5 fusion.13
  414.9 4.1 copy.318
  423.1 10.6 %while.39 = (s32[]{:T(128)}, f32[4,16]{1,0:T(4,128)S(1)}, f32[4,16,64,128]{3,2,1,0:T(8,128)S(1)}, f32[2,4,16]{2,1,0:T(4,128)S(1)}, f32[2,4,16,64,128]{4,3,2,1,0:...) while((s32[]{:T(128)}, f32[4,16]{1,0:T(4,128)S(1)}, ...), condition=%wide.region_12.13_spmd, body=%wide.region_10.12_spmd.sunk | while | flops 2097347 | bytes 29370552 | solution.py:78
  433.8 7.9 %fusion.11 = (f32[2,64,4,16]{1,3,2,0:T(8,128)}, f32[2,4,16,64,64]{4,3,2,1,0:T(8,128)S(1)}) fusion(f32[2,64,4,16,64]{1,4,3,2,0:T(8,128)} %copy.292, f32[2,4,16,64,128]{4,3,2,1,0:T(8,128)} %get-tuple-element.274, f32[2,64,4,128,1]{3,2,1,0,4:T(4,128)S(1)} %bitcast.263), kind=kOutput, calls=%fused_computation.27 | convolution fusion | flops 806346752 | bytes 8683520 | tf_op jit(solution)/shard_map/transpose(jvp(cqgrp,cqgn->cgrpn))/dot_general | solution.py:68
  441.7 7.9 %fusion.67 = f32[2,64,4,128]{3,1,2,0:T(8,128)} fusion(f32[2,4,16,64,128]{4,3,2,1,0:T(8,128)S(1)} %copy-done.12, f32[2,64,4,16,64]{1,4,3,2,0:T(8,128)S(1)} %copy-done.7, f32[2,64,4,16]{1,3,2,0:T(8,128)S(1)} %copy-done.37), kind=kOutput, calls=%fused_computation.104 | convolution fusion | flops 805830656 | bytes 6586368 | tf_op jit(solution)/shard_map/transpose(jvp(cqgrp,cqgn->cgrpn))/dot_general | solution.py:68
  449.7 5.8 fusion.10
  455.4 6.3 %copy.327 = f32[2,64,4,16,64]{4,3,2,1,0:T(8,128)} copy(f32[2,64,4,16,64]{1,4,3,2,0:T(8,128)} %fusion.10) | data formatting | bytes 4194304 | tf_op jit(solution)/shard_map/add | solution.py:216
  461.7 4.9 reshape.297
  469.6 5.0 multiply_reduce_fusion.4
  481.4 3.2 collective-permute-start.1
  491.8 24.6 %psum.15 = f32[3,64]{1,0:T(4,128)S(1)} all-reduce(f32[3,64]{1,0:T(4,128)S(1)} %pad_maximum_fusion.8), channel_id=1, replica_groups=mesh['groups'=2,'ctx'=16] {'ctx'}, use_global_device_ids=true, to_apply=%region_30.31 | all-reduce | flops 192 | bytes 1536 | tf_op jit(solution)/shard_map/psum | solution.py:230
  519.8 59.7 %all-reduce.33.cloned.1.call-done = f32[5,5120]{1,0:T(8,128)} async-done(((f32[5,5120]{1,0:T(8,128)}), f32[5,5120]{1,0:T(8,128)}) %all-reduce.33.cloned.1.call-update) | async-done | bytes 102416 | tf_op jit(solution)/shard_map/psum | solution.py:230
  (351 shorter events, 132.6 us)
Async XLA Ops:
  7.2 11.1 %copy-start.35 = (bf16[128,5120]{1,0:T(8,128)(2,1)S(1)}, bf16[128,5120]{1,0:T(8,128)(2,1)}, u32[]{:S(2)}) copy-start(bf16[128,5120]{1,0:T(8,128)(2,1)} %param.13) | copy-start | bytes 3932164
  8.8 9.5 %collective-permute-start = (bf16[3,5120]{1,0:T(4,128)(2,1)}, bf16[3,5120]{1,0:T(4,128)(2,1)}, u32[]{:S(2)}, u32[]{:S(2)}) collective-permute-start(bf16[3,5120]{1,0:T(4,128)(2,1)} %slice.256), channel_id=1, source_target_pairs={{0,1},{1,2},{2,3},{3,4},{4,5},{5,6},{6,7},{7,8},{8,9},{9,10},{10,1... | collective-permute-start | bytes 92168 | tf_op jit(solution)/shard_map/ppermute | solution.py:15
  12.4 7.1 %copy-start.71 = (f32[128]{0:T(128)}, f32[128]{0:T(128)S(1)}, u32[]{:S(2)}) copy-start(f32[128]{0:T(128)S(1)} %get-tuple-element.361) | copy-start | bytes 1540
  17.3 5.4 copy-start.49
  17.3 5.4 copy-start.51
  17.5 19.7 %copy-start.36 = (f32[2,64,4,16]{1,3,2,0:T(8,128)}, f32[2,64,4,16]{1,3,2,0:T(8,128)S(1)}, u32[]{:S(2)}) copy-start(f32[2,64,4,16]{1,3,2,0:T(8,128)S(1)} %copy_multiply_fusion) | copy-start | bytes 98308
  53.4 13.0 %copy-start.60 = (f32[2,4,16,1,1]{2,1,4,3,0:T(4,128)}, f32[2,4,16,1,1]{2,1,4,3,0:T(4,128)S(1)}, u32[]{:S(2)}) copy-start(f32[2,4,16,1,1]{2,1,4,3,0:T(4,128)S(1)} %get-tuple-element.577) | copy-start | bytes 1540
  54.1 12.3 %all-to-all-start.1 = ((f32[64,16,1]{0,2,1:T(1,128)}), f32[64,16,1]{0,2,1:T(1,128)S(1)}, u32[]{:S(2)}, u32[]{:S(2)}) async-start(f32[64,16,1]{0,2,1:T(1,128)} %broadcast_in_dim.115), calls=%async_computation.1 | async-start | bytes 16384 | tf_op jit(solution)/shard_map/all_to_all | solution.py:184
  66.4 52.3 %all-to-all-start = ((f32[64,16,512]{2,0,1:T(8,128)}), f32[64,16,512]{2,0,1:T(8,128)S(1)}, u32[]{:S(2)}, u32[]{:S(2)}) async-start(f32[64,16,512]{2,0,1:T(8,128)} %copy.300), calls=%async_computation | async-start | bytes 4194304 | tf_op jit(solution)/shard_map/all_to_all | solution.py:183
  120.2 8.5 %copy-start.79 = (f32[64,3,1]{0,1,2:T(4,128)S(1)}, f32[64,3,1]{0,1,2:T(4,128)}, u32[]{:S(2)}) copy-start(f32[64,3,1]{0,1,2:T(4,128)} %copy.423) | copy-start | bytes 2308
  124.2 10.7 %slice-start.1 = ((f32[64,8,512]{2,0,1:T(8,128)}), f32[64,1,512]{2,0,1:T(8,128)S(1)}, s32[]{:S(2)}) async-start(f32[64,8,512]{2,0,1:T(8,128)} %copy-done.26), calls=%async_computation.7 | async-start | bytes 262144 | tf_op jit(solution)/shard_map/slice | solution.py:118
  136.7 7.0 %copy-start.67 = (f32[64,7,1]{0,1,2:T(8,128)S(1)}, f32[64,7,1]{0,1,2:T(8,128)}, u32[]{:S(2)}) copy-start(f32[64,7,1]{0,1,2:T(8,128)} %copy.421) | copy-start | bytes 5380
  155.5 52.3 %all-to-all-start.2 = ((f32[64,16,512]{2,0,1:T(8,128)}), f32[64,16,512]{2,0,1:T(8,128)S(1)}, u32[]{:S(2)}, u32[]{:S(2)}) async-start(f32[64,16,512]{2,0,1:T(8,128)} %concatenate.38), calls=%async_computation.2 | async-start | bytes 4194304 | tf_op jit(solution)/shard_map/all_to_all | solution.py:188
  165.2 5.9 %copy-start.42 = (f32[128,512]{1,0:T(8,128)S(1)}, f32[128,512]{1,0:T(8,128)}, u32[]{:S(2)}) copy-start(f32[128,512]{1,0:T(8,128)} %get-tuple-element.371) | copy-start | bytes 786436
  217.0 10.0 %copy-start.13 = (f32[4,16,64,2,64]{4,2,1,0,3:T(8,128)}, f32[4,16,64,2,64]{4,2,1,0,3:T(8,128)S(1)}, u32[]{:S(2)}) copy-start(f32[4,16,64,2,64]{4,2,1,0,3:T(8,128)S(1)} %fusion.90) | copy-start | bytes 6291460
  217.0 10.0 %copy-start.31 = (f32[2,64,4,16]{1,3,2,0:T(8,128)S(1)}, f32[2,64,4,16]{1,3,2,0:T(8,128)}, u32[]{:S(2)}) copy-start(f32[2,64,4,16]{1,3,2,0:T(8,128)} %copy-done.30) | copy-start | bytes 98308
  217.0 10.0 %copy-start.69 = (f32[2,64]{1,0:T(2,128)S(1)}, f32[2,64]{1,0:T(2,128)}, u32[]{:S(2)}) copy-start(f32[2,64]{1,0:T(2,128)} %get-tuple-element.405) | copy-start | bytes 1540
  239.8 6.6 %copy-start.59 = (f32[64,8,1]{0,2,1:T(1,128)S(1)}, f32[64,8,1]{0,2,1:T(1,128)}, u32[]{:S(2)}) copy-start(f32[64,8,1]{0,2,1:T(1,128)} %get-tuple-element.394) | copy-start | bytes 6148
  239.8 6.6 %copy-start.68 = (f32[64,7,1]{0,2,1:T(1,128)S(1)}, f32[64,7,1]{0,2,1:T(1,128)}, u32[]{:S(2)}) copy-start(f32[64,7,1]{0,2,1:T(1,128)} %get-tuple-element.392) | copy-start | bytes 5380
  239.8 52.5 %all-to-all-start.3 = ((f32[64,16,512]{2,0,1:T(8,128)}), f32[64,16,512]{2,0,1:T(8,128)}, u32[]{:S(2)}, u32[]{:S(2)}) async-start(f32[64,16,512]{2,0,1:T(8,128)} %copy.317), calls=%async_computation.3 | async-start | bytes 4194304 | tf_op jit(solution)/shard_map/all_to_all | solution.py:202
  298.0 10.5 %slice-start = ((f32[64,8,512]{2,0,1:T(8,128)}), f32[64,1,512]{2,0,1:T(8,128)S(1)}, s32[]{:S(2)}) async-start(f32[64,8,512]{2,0,1:T(8,128)} %copy-done.25), calls=%async_computation.6 | async-start | bytes 262144 | tf_op jit(solution)/shard_map/slice | solution.py:118
  341.2 71.7 %all-to-all-start.4 = ((f32[64,16,512]{2,0,1:T(8,128)}), f32[64,16,512]{2,0,1:T(8,128)}, u32[]{:S(2)}, u32[]{:S(2)}) async-start(f32[64,16,512]{2,0,1:T(8,128)} %concatenate.42), calls=%async_computation.4 | async-start | bytes 4194304 | tf_op jit(solution)/shard_map/all_to_all | solution.py:207
  347.8 231.6 %all-reduce.33.cloned.1.call-start = ((), (), s32[]{:S(2)}) async-start(), calls=%async_computation.5 | async-start | bytes 327680 | tf_op jit(solution)/shard_map/psum | solution.py:230
  358.8 9.7 %copy-start.6 = (f32[2,64,4,16,64]{1,4,3,2,0:T(8,128)S(1)}, f32[2,64,4,16,64]{1,4,3,2,0:T(8,128)}, u32[]{:S(2)}) copy-start(f32[2,64,4,16,64]{1,4,3,2,0:T(8,128)} %copy.292) | copy-start | bytes 6291460
  358.8 9.7 %copy-start.14 = (f32[4,16,64,2,64]{4,2,1,0,3:T(8,128)S(1)}, f32[4,16,64,2,64]{4,2,1,0,3:T(8,128)}, u32[]{:S(2)}) copy-start(f32[4,16,64,2,64]{4,2,1,0,3:T(8,128)} %copy-done.13) | copy-start | bytes 6291460
  358.8 9.7 %copy-start.17 = (f32[2,4,16,64,64]{4,3,2,1,0:T(8,128)S(1)}, f32[2,4,16,64,64]{4,3,2,1,0:T(8,128)}, u32[]{:S(2)}) copy-start(f32[2,4,16,64,64]{4,3,2,1,0:T(8,128)} %get-tuple-element.410) | copy-start | bytes 6291460
  358.8 9.7 %copy-start.39 = (f32[2,64,4,16]{1,3,2,0:T(8,128)S(1)}, f32[2,64,4,16]{1,3,2,0:T(8,128)}, u32[]{:S(2)}) copy-start(f32[2,64,4,16]{1,3,2,0:T(8,128)} %copy-done.38) | copy-start | bytes 98308
  387.9 9.2 %copy-start.1 = (f32[2,64,4,16,64]{1,4,3,2,0:T(8,128)S(1)}, f32[2,64,4,16,64]{1,4,3,2,0:T(8,128)}, u32[]{:S(2)}) copy-start(f32[2,64,4,16,64]{1,4,3,2,0:T(8,128)} %copy.305) | copy-start | bytes 6291460
  397.1 8.9 %copy-start.40 = (f32[2,4,64,64]{3,2,1,0:T(8,128)S(1)}, f32[2,4,64,64]{3,2,1,0:T(8,128)}, u32[]{:S(2)}) copy-start(f32[2,4,64,64]{3,2,1,0:T(8,128)} %get-tuple-element.310) | copy-start | bytes 393220
  407.3 5.6 copy-start.16
  433.8 8.0 %copy-start.7 = (f32[2,64,4,16,64]{1,4,3,2,0:T(8,128)S(1)}, f32[2,64,4,16,64]{1,4,3,2,0:T(8,128)}, u32[]{:S(2)}) copy-start(f32[2,64,4,16,64]{1,4,3,2,0:T(8,128)} %copy.292) | copy-start | bytes 6291460
  433.8 7.9 %copy-start.12 = (f32[2,4,16,64,128]{4,3,2,1,0:T(8,128)S(1)}, f32[2,4,16,64,128]{4,3,2,1,0:T(8,128)}, u32[]{:S(2)}) copy-start(f32[2,4,16,64,128]{4,3,2,1,0:T(8,128)} %get-tuple-element.274) | copy-start | bytes 12582916
  433.8 7.9 %copy-start.37 = (f32[2,64,4,16]{1,3,2,0:T(8,128)S(1)}, f32[2,64,4,16]{1,3,2,0:T(8,128)}, u32[]{:S(2)}) copy-start(f32[2,64,4,16]{1,3,2,0:T(8,128)} %copy-done.36) | copy-start | bytes 98308
  441.7 7.9 %copy-start.2 = (f32[2,64,4,16,64]{1,4,3,2,0:T(8,128)S(1)}, f32[2,64,4,16,64]{1,4,3,2,0:T(8,128)}, u32[]{:S(2)}) copy-start(f32[2,64,4,16,64]{1,4,3,2,0:T(8,128)} %copy.305) | copy-start | bytes 6291460
  441.7 7.9 %copy-start.24 = (bf16[2,64,4,16,64]{1,4,3,2,0:T(8,128)(2,1)S(1)}, bf16[2,64,4,16,64]{1,4,3,2,0:T(8,128)(2,1)}, u32[]{:S(2)}) copy-start(bf16[2,64,4,16,64]{1,4,3,2,0:T(8,128)(2,1)} %copy.307) | copy-start | bytes 3145732
  461.7 7.8 %copy-start.4 = (f32[131,5120]{1,0:T(8,128)S(1)}, f32[131,5120]{1,0:T(8,128)}, u32[]{:S(2)}) copy-start(f32[131,5120]{1,0:T(8,128)} %copy-done.3) | copy-start | bytes 8048644
  479.1 5.6 copy-start.84
  479.1 6.5 %copy-start.34 = (f32[2,64,4,16]{1,0,3,2:T(2,128)S(1)}, f32[2,64,4,16]{1,0,3,2:T(2,128)}, u32[]{:S(2)}) copy-start(f32[2,64,4,16]{1,0,3,2:T(2,128)} %copy-done.32) | copy-start | bytes 98308
  479.1 6.5 %copy-start.45 = (f32[2,64,4,16]{1,3,2,0:T(8,128)S(1)}, f32[2,64,4,16]{1,3,2,0:T(8,128)}, u32[]{:S(2)}) copy-start(f32[2,64,4,16]{1,3,2,0:T(8,128)} %get-tuple-element.411) | copy-start | bytes 98308
  479.1 6.5 %copy-start.58 = (f32[2,4,16]{2,1,0:T(4,128)S(1)}, f32[2,4,16]{2,1,0:T(4,128)}, u32[]{:S(2)}) copy-start(f32[2,4,16]{2,1,0:T(4,128)} %copy-done.57) | copy-start | bytes 1540
  479.1 6.5 %copy-start.64 = (f32[2,64]{1,0:T(2,128)S(1)}, f32[2,64]{1,0:T(2,128)}, u32[]{:S(2)}) copy-start(f32[2,64]{1,0:T(2,128)} %copy-done.63) | copy-start | bytes 1540
  479.1 6.8 %copy-start.44 = (f32[2,64,4,16]{1,3,2,0:T(8,128)S(1)}, f32[2,64,4,16]{1,3,2,0:T(8,128)}, u32[]{:S(2)}) copy-start(f32[2,64,4,16]{1,3,2,0:T(8,128)} %copy-done.43) | copy-start | bytes 98308
  479.1 6.8 %copy-start.46 = (f32[2,64,4,16]{1,3,2,0:T(8,128)S(1)}, f32[2,64,4,16]{1,3,2,0:T(8,128)}, u32[]{:S(2)}) copy-start(f32[2,64,4,16]{1,3,2,0:T(8,128)} %get-tuple-element.311) | copy-start | bytes 98308
  479.1 6.8 %copy-start.70 = (f32[2,64]{1,0:T(2,128)S(1)}, f32[2,64]{1,0:T(2,128)}, u32[]{:S(2)}) copy-start(f32[2,64]{1,0:T(2,128)} %get-tuple-element.405) | copy-start | bytes 1540
  481.4 8.2 %copy-start.55 = (f32[128,64]{0,1:T(8,128)S(1)}, f32[128,64]{0,1:T(8,128)}, u32[]{:S(2)}) copy-start(f32[128,64]{0,1:T(8,128)} %param.14) | copy-start | bytes 98308
  481.4 8.2 %copy-start.80 = (f32[64]{0:T(128)S(1)}, f32[64]{0:T(128)}, u32[]{:S(2)}) copy-start(f32[64]{0:T(128)} %param.15) | copy-start | bytes 772
  481.4 8.2 %copy-start.82 = (f32[64]{0:T(128)S(1)}, f32[64]{0:T(128)}, u32[]{:S(2)}) copy-start(f32[64]{0:T(128)} %copy-done.81) | copy-start | bytes 772
  481.4 99.6 %collective-permute-start.1 = (f32[3,5120]{1,0:T(4,128)S(1)}, f32[3,5120]{1,0:T(4,128)S(1)}, u32[]{:S(2)}, u32[]{:S(2)}) collective-permute-start(f32[3,5120]{1,0:T(4,128)S(1)} %pad_add_fusion.3), channel_id=1, source_target_pairs={{1,0},{2,1},{3,2},{4,3},{5,4},{6,5},{7,6},{8,7},{9,8},{10,9},{11,1... | collective-permute-start | bytes 184328 | tf_op jit(solution)/shard_map/ppermute | solution.py:15
  (50 other events, 155.4 us)
Sparse Core Ops, SparseCore 0:
  489.7 89.6 all-reduce.32
where the time goes:
time: 601 us; the launch traced here: 591 us
  waiting for transfers between devices  185 us (31%)
  local copies, waits for them, and re-layouts  166 us (28%)
  matrix products  91.3 us (15%)
  other arithmetic  69.4 us (12%)
  starting transfers between devices  37.9 us (6%)
  blocking collectives  24.6 us (4%)
  between operations  15.6 us (3%)
    psum x1, waiting for transfers between devices, body(): lax.psum((jnp.concatenate([grad_kernel, grad_kernel_bias[None, :]], axis=...  59.7 us
    all_to_all x1, waiting for transfers between devices, body(): lax.all_to_all(flat_grads, 'ctx', split_axis=1, concat_axis=1, tiled=True)  45.7 us
    all_to_all x1, waiting for transfers between devices, body(): lax.all_to_all(flat_states, 'ctx', split_axis=1, concat_axis=1, tiled=True)  43.4 us
    all_to_all x2, waiting for transfers between devices, body(): lax.all_to_all(ready, 'ctx', split_axis=1, concat_axis=1, tiled=True)  36.5 us
    dot_general x3, matrix products, out_part(): y_diag = jnp.einsum('cgrts,csgrp->ctgrp', weights, inputs, precision=HIGH)  25 us
    psum x1, blocking collectives, body(): lax.psum((jnp.concatenate([grad_kernel, grad_kernel_bias[None, :]], axis=...  24.6 us
    dot_general x3, matrix products, out_part(): jnp.einsum('ctgn,cgrpn->ctgrp', c_values, b_chain, precision=HIGH)  24.4 us
    pad x8, local copies, waits for them, and re-layouts, owner_prefix(): lax.associative_scan(owner_join, (factors, values), reverse=reverse, axis=1)  22.9 us
  transfers between devices with their start and end apart: 8, of which 4 were waited for; matrix products, arithmetic and copies ran while one was open for 17% of the time, Pallas kernels for 0%

commit v1 on v0

--- a/solution.py
+++ b/solution.py
@@ -7,6 +7,12 @@
 
 GROUPS = 4
 HIGH = lax.Precision.HIGHEST
+
+
+def swap_blocks(x, axis, split, join):
+    pieces = jnp.split(x, lax.axis_size(axis), axis=split)
+    received = lax.all_to_all(jnp.stack(pieces), axis, 0, 0)
+    return jnp.concatenate(received, axis=join)
 
 
 def passed_along(value, axis, steps):
@@ -180,7 +186,7 @@
     flat_states = state_all.reshape(heads, devices, -1)
     ready = owner_prefix(
         (
-            lax.all_to_all(flat_states, "ctx", split_axis=1, concat_axis=1, tiled=True),
+            swap_blocks(flat_states, "ctx", 1, 1),
             lax.all_to_all(rates, "ctx", split_axis=1, concat_axis=1, tiled=True),
         ),
         False,

time: 601 us -> 623 us (1.037)
  local copies, waits for them, and re-layouts: 166 us -> 187 us
    unnamed x174 -> x191, local copies, waits for them, and re-layouts: 19 us -> 39.9 us
  transfers between devices with their start and end apart: 8 -> 8, of which waited for: 4 -> 5; matrix products, arithmetic and copies ran while one was open for 17% -> 16% of each run, Pallas kernels for 0% -> 0%
where the time goes in v1:
time: 623 us; the launch traced here: 612 us
  local copies, waits for them, and re-layouts  187 us (30%)
  waiting for transfers between devices  187 us (30%)
  matrix products  91.3 us (15%)
  other arithmetic  69.5 us (11%)
  starting transfers between devices  36.9 us (6%)
  blocking collectives  24.6 us (4%)
  between operations  15.7 us (3%)
    psum x1, waiting for transfers between devices, body(): lax.psum((jnp.concatenate([grad_kernel, grad_kernel_bias[None, :]], axis=...  59.6 us
    all_to_all x1, waiting for transfers between devices, body(): lax.all_to_all(flat_grads, 'ctx', split_axis=1, concat_axis=1, tiled=True)  45.7 us
    all_to_all x1, waiting for transfers between devices, swap_blocks(): received = lax.all_to_all(jnp.stack(pieces), axis, 0, 0)  43.4 us
    unnamed x191, local copies, waits for them, and re-layouts  39.9 us
    all_to_all x2, waiting for transfers between devices, body(): lax.all_to_all(ready, 'ctx', split_axis=1, concat_axis=1, tiled=True)  36.5 us
    dot_general x3, matrix products, out_part(): y_diag = jnp.einsum('cgrts,csgrp->ctgrp', weights, inputs, precision=HIGH)  25 us
    psum x1, blocking collectives, body(): lax.psum((jnp.concatenate([grad_kernel, grad_kernel_bias[None, :]], axis=...  24.6 us
    dot_general x3, matrix products, out_part(): jnp.einsum('ctgn,cgrpn->ctgrp', c_values, b_chain, precision=HIGH)  24.5 us
  transfers between devices with their start and end apart: 8, of which 5 were waited for; matrix products, arithmetic and copies ran while one was open for 16% of the time, Pallas kernels for 0%

profile of v1, /device:TPU:8, one launch (start us, length us, event | category | flops | bytes accessed | tf_op | source)
XLA Modules:
  0.0 612.1 jit_solution(13967640954085595676)
XLA Ops:
  19.5 3.2 fusion.41
  25.7 4.7 reshape.290
  30.4 5.8 copy.322
  37.3 7.0 %fusion.35 = f32[2,4,16,64,128]{4,3,2,1,0:T(8,128)} fusion(f32[2,64,4,16,64]{1,4,3,2,0:T(8,128)} %copy.322, f32[2,64,4,16]{1,3,2,0:T(8,128)S(1)} %copy_multiply_fusion, f32[2,64,4,128,1]{3,2,1,0,4:T(4,128)S(1)} %bitcast.332), kind=kOutput, calls=%fused_computation.60 | convolution fusion | flops 805830656 | bytes 6586368 | tf_op jit(solution)/shard_map/jvp(cqgrp,cqgn->cgrpn)/dot_general | solution.py:74
  46.8 6.6 %while.40 = (s32[]{:T(128)}, f32[4,16]{1,0:T(4,128)S(1)}, f32[4,16,64,128]{3,2,1,0:T(8,128)S(1)}, f32[2,4,16]{2,1,0:T(4,128)S(1)}, f32[2,4,16,64,128]{4,3,2,1,0:...) while((s32[]{:T(128)}, f32[4,16]{1,0:T(4,128)S(1)}, ...), condition=%wide.region_5.6_spmd.clone, body=%wide.region_4.5_spmd.clone.sunk | while | flops 2097347 | bytes 27272616 | solution.py:84
  76.0 6.6 %all-to-all-start.1 = ((f32[64,16,1]{0,2,1:T(1,128)}), f32[64,16,1]{0,2,1:T(1,128)S(1)}, u32[]{:S(2)}, u32[]{:S(2)}) async-start(f32[64,16,1]{0,2,1:T(1,128)} %broadcast_in_dim.115), calls=%async_computation.1 | async-start | bytes 16384 | tf_op jit(solution)/shard_map/all_to_all | solution.py:190
  87.4 5.6 all-to-all-start
  95.4 43.4 %all-to-all-done = f32[16,64,1,512]{3,1,2,0:T(8,128)S(1)} async-done(((f32[16,64,1,512]{3,1,2,0:T(8,128)}), f32[16,64,1,512]{3,1,2,0:T(8,128)S(1)}, u32[]{:S(2)}, u32[]{:S(2)}) %all-to-all-start) | async-done | bytes 2097184 | tf_op jit(solution)/shard_map/all_to_all | solution.py:14
  151.5 4.1 pad.96
  157.4 4.1 pad.95
  165.4 4.1 pad.143
  169.5 3.9 pad.221
  176.9 6.4 %all-to-all-start.2 = ((f32[64,16,512]{2,0,1:T(8,128)}), f32[64,16,512]{2,0,1:T(8,128)S(1)}, u32[]{:S(2)}, u32[]{:S(2)}) async-start(f32[64,16,512]{2,0,1:T(8,128)} %concatenate.38), calls=%async_computation.2 | async-start | bytes 4194304 | tf_op jit(solution)/shard_map/all_to_all | solution.py:194
  183.3 3.3 reshape.299
  186.6 5.9 copy.335
  192.7 36.5 %all-to-all-done.2 = f32[64,16,512]{2,0,1:T(8,128)S(1)} async-done(((f32[64,16,512]{2,0,1:T(8,128)}), f32[64,16,512]{2,0,1:T(8,128)S(1)}, u32[]{:S(2)}, u32[]{:S(2)}) %all-to-all-start.2) | async-done | bytes 2097184 | tf_op jit(solution)/shard_map/all_to_all | solution.py:194
  234.7 3.7 fusion.90
  238.4 10.0 %fusion.22 = (f32[2,64,4,16]{1,3,2,0:T(8,128)}, f32[2,64,4,16]{1,3,2,0:T(8,128)S(1)}, f32[2,4,16,64,64]{4,3,2,1,0:T(8,128)}) fusion(f32[2,64,4,16,64]{1,4,3,2,0:T(8,128)S(1)} %copy-done, f32[4,16,64,2,64]{4,2,1,0,3:T(8,128)S(1)} %fusion.90, f32[2,4,16,64,128]{4,3,2,1,0:T(8,128)} %get-tuple-element.578, f32[2,64,4,128,1]{3,2,1,0,4:T(4,128)S(1)} %bitcast.327), kind=kOutput, calls=%fused_computation.45 | convolution fusion | flops 807387136 | bytes 10813440 | tf_op jit(solution)/shard_map/jvp(ctgn,cgrpn->ctgrp)/dot_general | solution.py:103
  249.1 3.6 fusion.23
  257.1 4.1 copy.347
  261.2 6.6 %all-to-all-start.3 = ((f32[64,16,512]{2,0,1:T(8,128)}), f32[64,16,512]{2,0,1:T(8,128)}, u32[]{:S(2)}, u32[]{:S(2)}) async-start(f32[64,16,512]{2,0,1:T(8,128)} %copy.347), calls=%async_computation.3 | async-start | bytes 4194304 | tf_op jit(solution)/shard_map/all_to_all | solution.py:208
  267.9 45.7 %all-to-all-done.3 = f32[64,16,512]{2,0,1:T(8,128)} async-done(((f32[64,16,512]{2,0,1:T(8,128)}), f32[64,16,512]{2,0,1:T(8,128)}, u32[]{:S(2)}, u32[]{:S(2)}) %all-to-all-start.3) | async-done | bytes 2097184 | tf_op jit(solution)/shard_map/all_to_all | solution.py:208
  325.8 4.1 pad.105
  339.6 6.4 %pad.145 = f32[64,15,512]{2,0,1:T(8,128)} pad(f32[64,8,512]{2,0,1:T(8,128)} %pad_maximum_fusion.2, f32[]{:T(128)} %constant.116.clone.1), padding=0_0_0x0_0_1x0_0_0 | pad | bytes 3014660 | tf_op jit(solution)/shard_map/slice | solution.py:127
  346.0 6.5 %pad.222 = f32[64,16,512]{2,0,1:T(8,128)} pad(f32[64,8,512]{2,0,1:T(8,128)} %add.278, f32[]{:T(128)} %constant.116.clone.1), padding=0_0_0x1_0_1x0_0_0 | pad | bytes 3145732
  352.5 3.9 slice_add_fusion.7
  359.5 3.1 concatenate.42
  362.6 6.6 %all-to-all-start.4 = ((f32[64,16,512]{2,0,1:T(8,128)}), f32[64,16,512]{2,0,1:T(8,128)}, u32[]{:S(2)}, u32[]{:S(2)}) async-start(f32[64,16,512]{2,0,1:T(8,128)} %concatenate.42), calls=%async_computation.4 | async-start | bytes 4194304 | tf_op jit(solution)/shard_map/all_to_all | solution.py:213
  369.2 4.5 reshape.300
  373.9 4.9 copy.337
  380.2 9.7 %fusion.43 = (f32[2,4,16,64]{3,2,1,0:T(8,128)}, f32[2,4,16,64]{3,2,1,0:T(8,128)}, f32[2,4,16,64]{3,2,1,0:T(8,128)}, f32[2,4,64,64]{3,2,1,0:T(8,128)}) fusion(f32[2,4,16,64]{3,2,1,0:T(8,128)S(1)} %copy.321, f32[2,4,16,64]{3,2,1,0:T(8,128)S(1)} %copy.319, f32[2,4,64,64]{3,2,1,0:T(8,128)S(1)} %fusion.85, pred[2,64,64]{2,1,0:T(8,128)(4,1)S(1)} %compare_and_fusion, ...), kind=kOutput, calls=%fused_computation.79 | convolution fusion | flops 409411584 | bytes 3579904 | tf_op jit(solution)/shard_map/transpose(jvp(cgrts,csgrp->ctgrp))/dot_general | solution.py:101
  389.9 9.6 %fusion.18 = bf16[2,64,4,16,64]{1,4,3,2,0:T(8,128)(2,1)} fusion(f32[4,16,64,2,64]{4,2,1,0,3:T(8,128)S(1)} %copy-done.14, f32[2,4,16,64,64]{4,3,2,1,0:T(8,128)S(1)} %copy-done.17, f32[2,64,4,16,64]{1,4,3,2,0:T(8,128)S(1)} %copy-done.6, f32[2,64,4,16]{1,3,2,0:T(8,128)S(1)} %copy-done.39, f32[4,16]{1,0:T(4,128)S(1)} %mul.662, ...), kind=kOutput, calls=%fused_computation.39 | convolution fusion | flops 408420352 | bytes 7610624 | tf_op jit(solution)/shard_map/jvp(cgrts,csgrp->ctgrp)/dot_general | solution.py:101
  399.5 5.3 copy.334
  404.8 4.5 convert_element_type.79
  409.4 9.1 %convolution_bitcast_fusion.1 = f32[2,64,4,128]{3,1,2,0:T(8,128)S(1)} fusion(f32[4,16,64,128,1]{3,2,1,0,4:T(8,128)S(1)} %reshape.318, f32[2,64,4,16,64]{1,4,3,2,0:T(8,128)} %copy.335, f32[2,64,4,16]{1,3,2,0:T(8,128)S(1)} %copy-done.39), kind=kOutput, calls=%fused_computation.108 | convolution fusion | flops 805830656 | bytes 4489216 | tf_op jit(solution)/shard_map/transpose(jvp(ctgn,grpn->ctgrp))/dot_general | solution.py:111
  418.5 8.9 %fusion.70 = f32[2,4,64,128]{3,2,1,0:T(8,128)S(1)} fusion(f32[2,4,16,64,128]{4,3,2,1,0:T(8,128)} %get-tuple-element.578, f32[2,64,4,16,64]{1,4,3,2,0:T(8,128)S(1)} %copy-done.1, f32[2,64,4,16]{1,3,2,0:T(8,128)S(1)} %get-tuple-element.358), kind=kOutput, calls=%fused_computation.105 | convolution fusion | flops 805830656 | bytes 6586368 | tf_op jit(solution)/shard_map/transpose(jvp(ctgn,cgrpn->ctgrp))/dot_general | solution.py:103
  428.7 5.5 fusion.13
  436.3 4.1 copy.348
  444.6 10.6 %while.39 = (s32[]{:T(128)}, f32[4,16]{1,0:T(4,128)S(1)}, f32[4,16,64,128]{3,2,1,0:T(8,128)S(1)}, f32[2,4,16]{2,1,0:T(4,128)S(1)}, f32[2,4,16,64,128]{4,3,2,1,0:...) while((s32[]{:T(128)}, f32[4,16]{1,0:T(4,128)S(1)}, ...), condition=%wide.region_12.13_spmd, body=%wide.region_10.12_spmd.sunk | while | flops 2097347 | bytes 29370552 | solution.py:84
  455.3 7.9 %fusion.11 = (f32[2,64,4,16]{1,3,2,0:T(8,128)}, f32[2,4,16,64,64]{4,3,2,1,0:T(8,128)S(1)}) fusion(f32[2,64,4,16,64]{1,4,3,2,0:T(8,128)} %copy.322, f32[2,4,16,64,128]{4,3,2,1,0:T(8,128)} %get-tuple-element.274, f32[2,64,4,128,1]{3,2,1,0,4:T(4,128)S(1)} %bitcast.333), kind=kOutput, calls=%fused_computation.27 | convolution fusion | flops 806346752 | bytes 8683520 | tf_op jit(solution)/shard_map/transpose(jvp(cqgrp,cqgn->cgrpn))/dot_general | solution.py:74
  463.2 7.9 %fusion.67 = f32[2,64,4,128]{3,1,2,0:T(8,128)} fusion(f32[2,4,16,64,128]{4,3,2,1,0:T(8,128)S(1)} %copy-done.12, f32[2,64,4,16,64]{1,4,3,2,0:T(8,128)S(1)} %copy-done.7, f32[2,64,4,16]{1,3,2,0:T(8,128)S(1)} %copy-done.37), kind=kOutput, calls=%fused_computation.104 | convolution fusion | flops 805830656 | bytes 6586368 | tf_op jit(solution)/shard_map/transpose(jvp(cqgrp,cqgn->cgrpn))/dot_general | solution.py:74
  471.1 5.8 fusion.10
  476.9 6.3 %copy.357 = f32[2,64,4,16,64]{4,3,2,1,0:T(8,128)} copy(f32[2,64,4,16,64]{1,4,3,2,0:T(8,128)} %fusion.10) | data formatting | bytes 4194304 | tf_op jit(solution)/shard_map/add | solution.py:222
  483.1 4.9 reshape.305
  491.1 5.0 multiply_reduce_fusion.4
  502.8 3.2 collective-permute-start.1
  513.2 24.6 %psum.15 = f32[3,64]{1,0:T(4,128)S(1)} all-reduce(f32[3,64]{1,0:T(4,128)S(1)} %pad_maximum_fusion.8), channel_id=1, replica_groups=mesh['groups'=2,'ctx'=16] {'ctx'}, use_global_device_ids=true, to_apply=%region_30.31 | all-reduce | flops 192 | bytes 1536 | tf_op jit(solution)/shard_map/psum | solution.py:236
  541.2 59.6 %all-reduce.33.cloned.1.call-done = f32[5,5120]{1,0:T(8,128)} async-done(((f32[5,5120]{1,0:T(8,128)}), f32[5,5120]{1,0:T(8,128)}) %all-reduce.33.cloned.1.call-update) | async-done | bytes 102416 | tf_op jit(solution)/shard_map/psum | solution.py:236
  (369 shorter events, 156.1 us)
Async XLA Ops:
  7.2 11.1 %copy-start.35 = (bf16[128,5120]{1,0:T(8,128)(2,1)S(1)}, bf16[128,5120]{1,0:T(8,128)(2,1)}, u32[]{:S(2)}) copy-start(bf16[128,5120]{1,0:T(8,128)(2,1)} %param.13) | copy-start | bytes 3932164
  8.8 9.4 %collective-permute-start = (bf16[3,5120]{1,0:T(4,128)(2,1)}, bf16[3,5120]{1,0:T(4,128)(2,1)}, u32[]{:S(2)}, u32[]{:S(2)}) collective-permute-start(bf16[3,5120]{1,0:T(4,128)(2,1)} %slice.256), channel_id=1, source_target_pairs={{0,1},{1,2},{2,3},{3,4},{4,5},{5,6},{6,7},{7,8},{8,9},{9,10},{10,1... | collective-permute-start | bytes 92168 | tf_op jit(solution)/shard_map/ppermute | solution.py:21
  12.4 7.0 %copy-start.72 = (f32[128]{0:T(128)}, f32[128]{0:T(128)S(1)}, u32[]{:S(2)}) copy-start(f32[128]{0:T(128)S(1)} %get-tuple-element.361) | copy-start | bytes 1540
  17.3 5.3 copy-start.50
  17.3 5.3 copy-start.52
  17.6 19.7 %copy-start.36 = (f32[2,64,4,16]{1,3,2,0:T(8,128)}, f32[2,64,4,16]{1,3,2,0:T(8,128)S(1)}, u32[]{:S(2)}) copy-start(f32[2,64,4,16]{1,3,2,0:T(8,128)S(1)} %copy_multiply_fusion) | copy-start | bytes 98308
  53.4 6.9 %copy-start.61 = (f32[2,4,16,1,1]{2,1,4,3,0:T(4,128)}, f32[2,4,16,1,1]{2,1,4,3,0:T(4,128)S(1)}, u32[]{:S(2)}) copy-start(f32[2,4,16,1,1]{2,1,4,3,0:T(4,128)S(1)} %get-tuple-element.577) | copy-start | bytes 1540
  76.0 11.5 %all-to-all-start.1 = ((f32[64,16,1]{0,2,1:T(1,128)}), f32[64,16,1]{0,2,1:T(1,128)S(1)}, u32[]{:S(2)}, u32[]{:S(2)}) async-start(f32[64,16,1]{0,2,1:T(1,128)} %broadcast_in_dim.115), calls=%async_computation.1 | async-start | bytes 16384 | tf_op jit(solution)/shard_map/all_to_all | solution.py:190
  87.4 51.4 %all-to-all-start = ((f32[16,64,1,512]{3,1,2,0:T(8,128)}), f32[16,64,1,512]{3,1,2,0:T(8,128)S(1)}, u32[]{:S(2)}, u32[]{:S(2)}) async-start(f32[16,64,1,512]{3,1,2,0:T(8,128)} %copy.330), calls=%async_computation | async-start | bytes 4194304 | tf_op jit(solution)/shard_map/all_to_all | solution.py:14
  140.9 8.5 %copy-start.80 = (f32[64,3,1]{0,1,2:T(4,128)S(1)}, f32[64,3,1]{0,1,2:T(4,128)}, u32[]{:S(2)}) copy-start(f32[64,3,1]{0,1,2:T(4,128)} %copy.453) | copy-start | bytes 2308
  144.9 10.7 %slice-start.1 = ((f32[64,8,512]{2,0,1:T(8,128)}), f32[64,1,512]{2,0,1:T(8,128)S(1)}, s32[]{:S(2)}) async-start(f32[64,8,512]{2,0,1:T(8,128)} %copy-done.26), calls=%async_computation.7 | async-start | bytes 262144 | tf_op jit(solution)/shard_map/slice | solution.py:124
  157.4 7.0 %copy-start.68 = (f32[64,7,1]{0,1,2:T(8,128)S(1)}, f32[64,7,1]{0,1,2:T(8,128)}, u32[]{:S(2)}) copy-start(f32[64,7,1]{0,1,2:T(8,128)} %copy.451) | copy-start | bytes 5380
  176.9 52.3 %all-to-all-start.2 = ((f32[64,16,512]{2,0,1:T(8,128)}), f32[64,16,512]{2,0,1:T(8,128)S(1)}, u32[]{:S(2)}, u32[]{:S(2)}) async-start(f32[64,16,512]{2,0,1:T(8,128)} %concatenate.38), calls=%async_computation.2 | async-start | bytes 4194304 | tf_op jit(solution)/shard_map/all_to_all | solution.py:194
  186.6 5.9 copy-start.42
  238.4 10.1 %copy-start.13 = (f32[4,16,64,2,64]{4,2,1,0,3:T(8,128)}, f32[4,16,64,2,64]{4,2,1,0,3:T(8,128)S(1)}, u32[]{:S(2)}) copy-start(f32[4,16,64,2,64]{4,2,1,0,3:T(8,128)S(1)} %fusion.90) | copy-start | bytes 6291460
  238.4 10.0 %copy-start.31 = (f32[2,64,4,16]{1,3,2,0:T(8,128)S(1)}, f32[2,64,4,16]{1,3,2,0:T(8,128)}, u32[]{:S(2)}) copy-start(f32[2,64,4,16]{1,3,2,0:T(8,128)} %copy-done.30) | copy-start | bytes 98308
  238.4 10.0 %copy-start.70 = (f32[2,64]{1,0:T(2,128)S(1)}, f32[2,64]{1,0:T(2,128)}, u32[]{:S(2)}) copy-start(f32[2,64]{1,0:T(2,128)} %get-tuple-element.405) | copy-start | bytes 1540
  261.2 6.6 %copy-start.60 = (f32[64,8,1]{0,2,1:T(1,128)S(1)}, f32[64,8,1]{0,2,1:T(1,128)}, u32[]{:S(2)}) copy-start(f32[64,8,1]{0,2,1:T(1,128)} %get-tuple-element.394) | copy-start | bytes 6148
  261.2 6.6 %copy-start.69 = (f32[64,7,1]{0,2,1:T(1,128)S(1)}, f32[64,7,1]{0,2,1:T(1,128)}, u32[]{:S(2)}) copy-start(f32[64,7,1]{0,2,1:T(1,128)} %get-tuple-element.392) | copy-start | bytes 5380
  261.2 52.5 %all-to-all-start.3 = ((f32[64,16,512]{2,0,1:T(8,128)}), f32[64,16,512]{2,0,1:T(8,128)}, u32[]{:S(2)}, u32[]{:S(2)}) async-start(f32[64,16,512]{2,0,1:T(8,128)} %copy.347), calls=%async_computation.3 | async-start | bytes 4194304 | tf_op jit(solution)/shard_map/all_to_all | solution.py:208
  319.4 10.5 %slice-start = ((f32[64,8,512]{2,0,1:T(8,128)}), f32[64,1,512]{2,0,1:T(8,128)S(1)}, s32[]{:S(2)}) async-start(f32[64,8,512]{2,0,1:T(8,128)} %copy-done.25), calls=%async_computation.6 | async-start | bytes 262144 | tf_op jit(solution)/shard_map/slice | solution.py:124
  362.6 71.7 %all-to-all-start.4 = ((f32[64,16,512]{2,0,1:T(8,128)}), f32[64,16,512]{2,0,1:T(8,128)}, u32[]{:S(2)}, u32[]{:S(2)}) async-start(f32[64,16,512]{2,0,1:T(8,128)} %concatenate.42), calls=%async_computation.4 | async-start | bytes 4194304 | tf_op jit(solution)/shard_map/all_to_all | solution.py:213
  369.2 231.7 %all-reduce.33.cloned.1.call-start = ((), (), s32[]{:S(2)}) async-start(), calls=%async_computation.5 | async-start | bytes 327680 | tf_op jit(solution)/shard_map/psum | solution.py:236
  380.2 9.7 %copy-start.6 = (f32[2,64,4,16,64]{1,4,3,2,0:T(8,128)S(1)}, f32[2,64,4,16,64]{1,4,3,2,0:T(8,128)}, u32[]{:S(2)}) copy-start(f32[2,64,4,16,64]{1,4,3,2,0:T(8,128)} %copy.322) | copy-start | bytes 6291460
  380.2 9.7 %copy-start.14 = (f32[4,16,64,2,64]{4,2,1,0,3:T(8,128)S(1)}, f32[4,16,64,2,64]{4,2,1,0,3:T(8,128)}, u32[]{:S(2)}) copy-start(f32[4,16,64,2,64]{4,2,1,0,3:T(8,128)} %copy-done.13) | copy-start | bytes 6291460
  380.2 9.7 %copy-start.17 = (f32[2,4,16,64,64]{4,3,2,1,0:T(8,128)S(1)}, f32[2,4,16,64,64]{4,3,2,1,0:T(8,128)}, u32[]{:S(2)}) copy-start(f32[2,4,16,64,64]{4,3,2,1,0:T(8,128)} %get-tuple-element.410) | copy-start | bytes 6291460
  380.2 9.7 %copy-start.39 = (f32[2,64,4,16]{1,3,2,0:T(8,128)S(1)}, f32[2,64,4,16]{1,3,2,0:T(8,128)}, u32[]{:S(2)}) copy-start(f32[2,64,4,16]{1,3,2,0:T(8,128)} %copy-done.38) | copy-start | bytes 98308
  409.3 9.2 %copy-start.1 = (f32[2,64,4,16,64]{1,4,3,2,0:T(8,128)S(1)}, f32[2,64,4,16,64]{1,4,3,2,0:T(8,128)}, u32[]{:S(2)}) copy-start(f32[2,64,4,16,64]{1,4,3,2,0:T(8,128)} %copy.335) | copy-start | bytes 6291460
  418.5 8.9 %copy-start.40 = (f32[2,4,64,64]{3,2,1,0:T(8,128)S(1)}, f32[2,4,64,64]{3,2,1,0:T(8,128)}, u32[]{:S(2)}) copy-start(f32[2,4,64,64]{3,2,1,0:T(8,128)} %get-tuple-element.310) | copy-start | bytes 393220
  428.7 5.6 copy-start.16
  455.2 8.0 %copy-start.7 = (f32[2,64,4,16,64]{1,4,3,2,0:T(8,128)S(1)}, f32[2,64,4,16,64]{1,4,3,2,0:T(8,128)}, u32[]{:S(2)}) copy-start(f32[2,64,4,16,64]{1,4,3,2,0:T(8,128)} %copy.322) | copy-start | bytes 6291460
  455.2 8.0 %copy-start.12 = (f32[2,4,16,64,128]{4,3,2,1,0:T(8,128)S(1)}, f32[2,4,16,64,128]{4,3,2,1,0:T(8,128)}, u32[]{:S(2)}) copy-start(f32[2,4,16,64,128]{4,3,2,1,0:T(8,128)} %get-tuple-element.274) | copy-start | bytes 12582916
  455.2 8.0 %copy-start.37 = (f32[2,64,4,16]{1,3,2,0:T(8,128)S(1)}, f32[2,64,4,16]{1,3,2,0:T(8,128)}, u32[]{:S(2)}) copy-start(f32[2,64,4,16]{1,3,2,0:T(8,128)} %copy-done.36) | copy-start | bytes 98308
  463.2 7.9 %copy-start.2 = (f32[2,64,4,16,64]{1,4,3,2,0:T(8,128)S(1)}, f32[2,64,4,16,64]{1,4,3,2,0:T(8,128)}, u32[]{:S(2)}) copy-start(f32[2,64,4,16,64]{1,4,3,2,0:T(8,128)} %copy.335) | copy-start | bytes 6291460
  463.2 7.9 %copy-start.24 = (bf16[2,64,4,16,64]{1,4,3,2,0:T(8,128)(2,1)S(1)}, bf16[2,64,4,16,64]{1,4,3,2,0:T(8,128)(2,1)}, u32[]{:S(2)}) copy-start(bf16[2,64,4,16,64]{1,4,3,2,0:T(8,128)(2,1)} %copy.337) | copy-start | bytes 3145732
  483.1 7.8 %copy-start.4 = (f32[131,5120]{1,0:T(8,128)S(1)}, f32[131,5120]{1,0:T(8,128)}, u32[]{:S(2)}) copy-start(f32[131,5120]{1,0:T(8,128)} %copy-done.3) | copy-start | bytes 8048644
  500.5 5.6 copy-start.85
  500.5 6.5 %copy-start.34 = (f32[2,64,4,16]{1,0,3,2:T(2,128)S(1)}, f32[2,64,4,16]{1,0,3,2:T(2,128)}, u32[]{:S(2)}) copy-start(f32[2,64,4,16]{1,0,3,2:T(2,128)} %copy-done.32) | copy-start | bytes 98308
  500.5 6.5 %copy-start.45 = (f32[2,64,4,16]{1,3,2,0:T(8,128)S(1)}, f32[2,64,4,16]{1,3,2,0:T(8,128)}, u32[]{:S(2)}) copy-start(f32[2,64,4,16]{1,3,2,0:T(8,128)} %get-tuple-element.411) | copy-start | bytes 98308
  500.5 6.5 %copy-start.59 = (f32[2,4,16]{2,1,0:T(4,128)S(1)}, f32[2,4,16]{2,1,0:T(4,128)}, u32[]{:S(2)}) copy-start(f32[2,4,16]{2,1,0:T(4,128)} %copy-done.58) | copy-start | bytes 1540
  500.5 6.5 %copy-start.65 = (f32[2,64]{1,0:T(2,128)S(1)}, f32[2,64]{1,0:T(2,128)}, u32[]{:S(2)}) copy-start(f32[2,64]{1,0:T(2,128)} %copy-done.64) | copy-start | bytes 1540
  500.5 6.8 %copy-start.44 = (f32[2,64,4,16]{1,3,2,0:T(8,128)S(1)}, f32[2,64,4,16]{1,3,2,0:T(8,128)}, u32[]{:S(2)}) copy-start(f32[2,64,4,16]{1,3,2,0:T(8,128)} %copy-done.43) | copy-start | bytes 98308
  500.5 6.8 %copy-start.47 = (f32[2,64,4,16]{1,3,2,0:T(8,128)S(1)}, f32[2,64,4,16]{1,3,2,0:T(8,128)}, u32[]{:S(2)}) copy-start(f32[2,64,4,16]{1,3,2,0:T(8,128)} %get-tuple-element.311) | copy-start | bytes 98308
  500.6 6.8 %copy-start.71 = (f32[2,64]{1,0:T(2,128)S(1)}, f32[2,64]{1,0:T(2,128)}, u32[]{:S(2)}) copy-start(f32[2,64]{1,0:T(2,128)} %get-tuple-element.405) | copy-start | bytes 1540
  502.8 8.2 %copy-start.56 = (f32[128,64]{0,1:T(8,128)S(1)}, f32[128,64]{0,1:T(8,128)}, u32[]{:S(2)}) copy-start(f32[128,64]{0,1:T(8,128)} %param.14) | copy-start | bytes 98308
  502.8 8.2 %copy-start.81 = (f32[64]{0:T(128)S(1)}, f32[64]{0:T(128)}, u32[]{:S(2)}) copy-start(f32[64]{0:T(128)} %param.15) | copy-start | bytes 772
  502.8 8.2 %copy-start.83 = (f32[64]{0:T(128)S(1)}, f32[64]{0:T(128)}, u32[]{:S(2)}) copy-start(f32[64]{0:T(128)} %copy-done.82) | copy-start | bytes 772
  502.8 99.6 %collective-permute-start.1 = (f32[3,5120]{1,0:T(4,128)S(1)}, f32[3,5120]{1,0:T(4,128)S(1)}, u32[]{:S(2)}, u32[]{:S(2)}) collective-permute-start(f32[3,5120]{1,0:T(4,128)S(1)} %pad_add_fusion.3), channel_id=1, source_target_pairs={{1,0},{2,1},{3,2},{4,3},{5,4},{6,5},{7,6},{8,7},{9,8},{10,9},{11,1... | collective-permute-start | bytes 184328 | tf_op jit(solution)/shard_map/ppermute | solution.py:21
  (51 other events, 156.0 us)
Sparse Core Ops, SparseCore 0:
  511.2 89.6 all-reduce.32
